TPU v7x, 256 devices: a whole 4x4x8 slice. The times are simulated.
256 devices in a mesh: row: 8 (over x, core), col: 32 (over z, y).
Axes of the slice: x: 4, y: 4, z: 8, core: 2. Of those that a mesh axis runs over, the one named last changes fastest.
Arguments:
- matrix: float32 [24576, 12288], P('row', 'col'), may hold values from -6 to 6
Outputs:
- updated: float32 [24576, 12288], P('row', 'col')
All inputs are finite; a program needn't handle non-finite values.
Results may differ from a plain program's by a relative error of at most 0.0003.
Values sent between devices are 32-bit elements; how exact they have to be, the bound alone decides.
A program may use at most 64 MiB of HBM per device.

v0:
```python
import jax
import jax.numpy as jnp
from jax import lax
from jax.sharding import PartitionSpec as P

PANEL = 256
HIGHEST = lax.Precision.HIGHEST


def partner_2(block, axis, distance):
    count = lax.axis_size(axis)
    route = []
    for low in range(count):
        high = low | 1 << distance
        if high != low and high < count:
            route += [(low, high), (high, low)]
    return lax.ppermute(block, axis, route)


def broadcast(value, axis, source):
    kept = jnp.where(lax.axis_index(axis) == source, value, 0).astype(value.dtype)
    return lax.psum(kept, axis)


def upper_of(gram):
    return jnp.linalg.cholesky(gram).T


def combine_pair(upper_one, upper_two):
    gram = jnp.dot(upper_one.T, upper_one, precision=HIGHEST) + jnp.dot(
        upper_two.T, upper_two, precision=HIGHEST
    )
    return upper_of(gram)


def apply_inverse(upper, rows):
    return jax.scipy.linalg.solve_triangular(upper.T, rows.T, lower=True).T


def factor(panel):
    gram_local = lax.dot_general(panel, panel, (((0,), (0,)), ((), ())), precision=HIGHEST)
    is_first = lax.axis_index("row") == 0
    identity = jnp.eye(PANEL, dtype=jnp.float32)
    upper = upper_of(gram_local)
    for level in range(lax.axis_size("row").bit_length() - 1):
        partner = partner_2(upper, "row", level)
        upper = combine_pair(upper, partner)
    basis = apply_inverse(upper, panel)
    top_block = broadcast(basis[:PANEL], "row", 0)
    lead = identity + top_block
    vectors = basis.at[:PANEL].add(jnp.where(is_first, identity, jnp.zeros_like(identity)))
    return (vectors, lead)


def on_device(matrix):
    panel = matrix[:, :PANEL]
    vectors, lead = factor(panel)
    vectors, lead = (broadcast(vectors, "col", 0), broadcast(lead, "col", 0))
    partial_proj = lax.dot_general(vectors, matrix, (((0,), (0,)), ((), ())), precision=HIGHEST)
    projected = lax.psum(partial_proj, "row")
    lead_gram = jnp.dot(lead.T, lead, precision=HIGHEST)
    lead_factor = jnp.linalg.cholesky(lead_gram)
    coeffs = jax.scipy.linalg.cho_solve(
        (lead_factor, True), jnp.dot(lead.T, projected, precision=HIGHEST)
    )
    return matrix - jnp.dot(vectors, coeffs, precision=HIGHEST)


def solution(mesh):
    in_specs = (P("row", "col"),)
    out_specs = P("row", "col")
    return jax.shard_map(
        on_device, mesh=mesh, in_specs=in_specs, out_specs=out_specs, check_vma=False
    )
```

profile of v0, /device:TPU:8, one launch (start us, length us, event | category | flops | bytes accessed | tf_op | source)
XLA Modules:
  0.0 583.5 jit_solution(9986484635231155321)
XLA Ops:
  6.5 7.9 %fusion.1 = f32[256,256]{1,0:T(8,128)S(1)} fusion(f32[3072,384]{1,0:T(8,128)} %param.4), kind=kOutput, calls=%fused_computation.11 | convolution fusion | flops 2415919104 | bytes 3407872 | tf_op jit(solution)/shard_map/dot_general | solution.py:41
  14.7 11.7 %cholesky.256 = f32[128,128]{1,0:T(8,128)S(1)} custom-call(f32[128,128]{1,0:T(8,128)S(1)} %cholesky.422), custom_call_target="Cholesky" | custom-call | tf_op jit(solution)/shard_map/jit(cholesky)/cholesky | solution.py:26
  26.4 9.8 %custom-call.25 = f32[1,128,128]{1,2,0:T(8,128)S(1)} custom-call(f32[1,128,128]{2,1,0:T(8,128)S(1)} %get-tuple-element.77), custom_call_target="InvertDiagBlocksLowerTriangular" | custom-call | tf_op jit(solution)/shard_map/jit(cholesky)/cholesky | solution.py:26
  36.8 11.9 %cholesky.273 = f32[128,128]{1,0:T(8,128)S(1)} custom-call(f32[128,128]{1,0:T(8,128)S(1)} %convolution_subtract_fusion.5), custom_call_target="Cholesky" | custom-call | tf_op jit(solution)/shard_map/jit(cholesky)/cholesky | solution.py:26
  51.3 1.1 collective-permute-done
  53.0 11.7 %cholesky.290 = f32[128,128]{1,0:T(8,128)S(1)} custom-call(f32[128,128]{1,0:T(8,128)S(1)} %cholesky.425), custom_call_target="Cholesky" | custom-call | tf_op jit(solution)/shard_map/jit(cholesky)/cholesky | solution.py:26
  64.8 9.8 %custom-call.26 = f32[1,128,128]{1,2,0:T(8,128)S(1)} custom-call(f32[1,128,128]{2,1,0:T(8,128)S(1)} %get-tuple-element.73), custom_call_target="InvertDiagBlocksLowerTriangular" | custom-call | tf_op jit(solution)/shard_map/jit(cholesky)/cholesky | solution.py:26
  75.1 11.7 %cholesky.307 = f32[128,128]{1,0:T(8,128)S(1)} custom-call(f32[128,128]{1,0:T(8,128)S(1)} %slice_subtract_fusion.2), custom_call_target="Cholesky" | custom-call | tf_op jit(solution)/shard_map/jit(cholesky)/cholesky | solution.py:26
  89.6 2.0 collective-permute-start.1
  91.6 3.8 slice_bitcast_fusion
  95.7 2.7 collective-permute-done.1
  99.0 11.7 %cholesky.324 = f32[128,128]{1,0:T(8,128)S(1)} custom-call(f32[128,128]{1,0:T(8,128)S(1)} %cholesky.428), custom_call_target="Cholesky" | custom-call | tf_op jit(solution)/shard_map/jit(cholesky)/cholesky | solution.py:26
  110.8 9.8 %custom-call.27 = f32[1,128,128]{1,2,0:T(8,128)S(1)} custom-call(f32[1,128,128]{2,1,0:T(8,128)S(1)} %get-tuple-element.69), custom_call_target="InvertDiagBlocksLowerTriangular" | custom-call | tf_op jit(solution)/shard_map/jit(cholesky)/cholesky | solution.py:26
  121.1 11.7 %cholesky.341 = f32[128,128]{1,0:T(8,128)S(1)} custom-call(f32[128,128]{1,0:T(8,128)S(1)} %slice_subtract_fusion.1), custom_call_target="Cholesky" | custom-call | tf_op jit(solution)/shard_map/jit(cholesky)/cholesky | solution.py:26
  135.5 3.3 collective-permute-start.2
  139.2 5.6 collective-permute-done.2
  145.3 11.7 %cholesky.358 = f32[128,128]{1,0:T(8,128)S(1)} custom-call(f32[128,128]{1,0:T(8,128)S(1)} %cholesky.431), custom_call_target="Cholesky" | custom-call | tf_op jit(solution)/shard_map/jit(cholesky)/cholesky | solution.py:26
  157.1 9.8 %custom-call.28 = f32[1,128,128]{1,2,0:T(8,128)S(1)} custom-call(f32[1,128,128]{2,1,0:T(8,128)S(1)} %get-tuple-element.65), custom_call_target="InvertDiagBlocksLowerTriangular" | custom-call | tf_op jit(solution)/shard_map/jit(cholesky)/cholesky | solution.py:26
  167.4 11.7 %cholesky.375 = f32[128,128]{1,0:T(8,128)S(1)} custom-call(f32[128,128]{1,0:T(8,128)S(1)} %slice_subtract_fusion), custom_call_target="Cholesky" | custom-call | tf_op jit(solution)/shard_map/jit(cholesky)/cholesky | solution.py:26
  181.8 4.0 while.3
  182.6 1.3 bitcast_dynamic-update-slice_fusion.4
  184.5 1.3 bitcast_dynamic-update-slice_fusion.4
  185.8 19.7 %custom-call.19 = f32[2,128,128]{1,2,0:T(8,128)S(1)} custom-call(f32[2,128,128]{2,1,0:T(8,128)S(1)} %get-tuple-element.25), custom_call_target="InvertDiagBlocksLowerTriangular" | custom-call | tf_op jit(solution)/shard_map/jit(_solve_triangular)/triangular_solve | solution.py:37
  205.5 2.9 fusion.3
  208.4 5.2 convolution_subtract_fusion.1
  214.0 2.8 fusion.38
  217.9 1.7 copy-done
  219.6 1.9 broadcast_select_fusion
  221.5 66.5 %all-reduce.6.cloned.1.call-done = f32[256,256]{1,0:T(8,128)} async-done(((f32[256,256]{1,0:T(8,128)}), f32[256,256]{1,0:T(8,128)}) %all-reduce.6.cloned.1.call-update) | async-done | bytes 262160 | tf_op jit(solution)/shard_map/psum | solution.py:22
  287.9 1.7 fusion.10
  290.1 159.1 %all-reduce.10.cloned.1.call-done = (f32[3072,256]{1,0:T(8,128)}, f32[256,256]{1,0:T(8,128)}) async-done(((f32[3072,256]{1,0:T(8,128)}, f32[256,256]{1,0:T(8,128)}), (f32[3072,256]{1,0:T(8,128)}, f32[256,256]{1,0:T(8,128)})) %all-reduce.10.cloned.1.call-update) | async-done | bytes 3407888 | tf_op jit(solution)/shard_map/psum | solution.py:22
  449.2 1.8 fusion.78
  453.6 11.7 %cholesky.392 = f32[128,128]{1,0:T(8,128)S(1)} custom-call(f32[128,128]{1,0:T(8,128)S(1)} %cholesky.434), custom_call_target="Cholesky" | custom-call | tf_op jit(solution)/shard_map/jit(cholesky)/cholesky | solution.py:62
  465.3 9.8 %custom-call.29 = f32[1,128,128]{1,2,0:T(8,128)S(1)} custom-call(f32[1,128,128]{2,1,0:T(8,128)S(1)} %get-tuple-element.61), custom_call_target="InvertDiagBlocksLowerTriangular" | custom-call | tf_op jit(solution)/shard_map/jit(cholesky)/cholesky | solution.py:62
  475.1 1.0 constant_dynamic-update-slice_fusion.1
  476.2 1.1 convolution_subtract_fusion.4
  477.3 11.7 %cholesky.409 = f32[128,128]{1,0:T(8,128)S(1)} custom-call(f32[128,128]{1,0:T(8,128)S(1)} %convolution_subtract_fusion.4), custom_call_target="Cholesky" | custom-call | tf_op jit(solution)/shard_map/jit(cholesky)/cholesky | solution.py:62
  490.5 8.0 %fusion.79 = f32[256,384]{1,0:T(8,128)} fusion(f32[3072,256]{1,0:T(8,128)S(1)} %copy-done.1, f32[3072,384]{1,0:T(8,128)} %param.4), kind=kOutput, calls=%fused_computation.151 | convolution fusion | flops 3623878656 | bytes 8257536 | tf_op jit(solution)/shard_map/dot_general | solution.py:59
  499.8 1.7 select_select_fusion
  501.5 5.7 while.4
  502.1 2.2 bitcast_dynamic-update-slice_fusion.5
  505.0 2.2 bitcast_dynamic-update-slice_fusion.5
  507.8 20.5 %custom-call.20 = f32[2,128,128]{1,2,0:T(8,128)S(1)} custom-call(f32[2,128,128]{2,1,0:T(8,128)} %copy-done.5), custom_call_target="InvertDiagBlocksLowerTriangular" | custom-call | tf_op jit(solution)/shard_map/jit(_cho_solve)/triangular_solve | solution.py:63
  528.3 34.7 %all-reduce.8.cloned.1.call-done = f32[256,384]{1,0:T(8,128)} async-done(((f32[256,384]{1,0:T(8,128)}), f32[256,384]{1,0:T(8,128)}) %all-reduce.8.cloned.1.call-update) | async-done | bytes 393232 | tf_op jit(solution)/shard_map/psum | solution.py:60
  563.0 1.6 fusion.80
  565.0 1.2 convolution_subtract_fusion.3
  566.9 1.2 convolution_subtract_fusion.2
  568.4 8.4 %convolution_subtract_fusion = f32[3072,384]{1,0:T(8,128)} fusion(f32[3072,384]{1,0:T(8,128)} %param.4, f32[3072,256]{1,0:T(8,128)S(1)} %copy-done.1, f32[128,384]{1,0:T(8,128)S(1)} %fusion.65, f32[128,384]{1,0:T(8,128)S(1)} %fusion.64), kind=kOutput, calls=%fused_computation.4 | convolution fusion | flops 3625156608 | bytes 12976128 | tf_op jit(solution)/shard_map/dot_general | solution.py:66
  (94 shorter events, 20.8 us)
Async XLA Ops:
  6.5 281.4 %all-reduce.6.cloned.1.call-start = ((), (), s32[]{:S(2)}) async-start(), calls=%async_computation | async-start | bytes 524288 | tf_op jit(solution)/shard_map/psum | solution.py:22
  50.8 1.6 collective-permute-start
  89.6 8.8 %collective-permute-start.1 = (f32[256,256]{0,1:T(8,128)S(1)}, f32[256,256]{0,1:T(8,128)S(1)}, u32[]{:S(2)}, u32[]{:S(2)}) collective-permute-start(f32[256,256]{0,1:T(8,128)S(1)} %fusion.20), channel_id=1, source_target_pairs={{0,64},{64,0},{32,96},{96,32},{128,192},{192,128},{160,224},{224,1... | collective-permute-start | bytes 786440 | tf_op jit(solution)/shard_map/ppermute | solution.py:17
  135.5 9.3 %collective-permute-start.2 = (f32[256,256]{0,1:T(8,128)S(1)}, f32[256,256]{0,1:T(8,128)S(1)}, u32[]{:S(2)}, u32[]{:S(2)}) collective-permute-start(f32[256,256]{0,1:T(8,128)S(1)} %fusion.22), channel_id=1, source_target_pairs={{0,128},{128,0},{32,160},{160,32},{64,192},{192,64},{96,224},{224,... | collective-permute-start | bytes 786440 | tf_op jit(solution)/shard_map/ppermute | solution.py:17
  217.9 1.7 copy-start
  219.5 229.7 %all-reduce.10.cloned.1.call-start = ((), (), s32[]{:S(2)}) async-start(), calls=%async_computation.2 | async-start | bytes 6815744 | tf_op jit(solution)/shard_map/psum | solution.py:22
  289.7 273.3 %all-reduce.8.cloned.1.call-start = ((), (), s32[]{:S(2)}) async-start(), calls=%async_computation.1 | async-start | bytes 786432 | tf_op jit(solution)/shard_map/psum | solution.py:60
  449.2 41.2 %copy-start.1 = (f32[3072,256]{1,0:T(8,128)S(1)}, f32[3072,256]{1,0:T(8,128)}, u32[]{:S(2)}) copy-start(f32[3072,256]{1,0:T(8,128)} %get-tuple-element.50) | copy-start | bytes 9437188
  452.8 0.7 copy-start.4
  489.1 1.4 copy-start.3
  490.5 72.5 %copy-start.2 = (f32[256,256]{1,0:T(8,128)S(1)}, f32[256,256]{1,0:T(8,128)}, u32[]{:S(2)}) copy-start(f32[256,256]{1,0:T(8,128)} %get-tuple-element.51) | copy-start | bytes 786436
  507.2 0.6 copy-start.5
Sparse Core Ops, SparseCore 0:
  219.7 68.2 all-reduce.5
  291.6 157.5 all-reduce.9
  498.6 64.3 all-reduce.7
where the time goes:
time: 593 us; the launch traced here: 583 us
  waiting for transfers between devices  270 us (46%)
  other arithmetic  220 us (37%)
  matrix products  48.8 us (8%)
  between operations  20.2 us (3%)
  local copies, waits for them, and re-layouts  18.1 us (3%)
    psum x2, waiting for transfers between devices, broadcast(): return lax.psum(kept, axis)  226 us
    another operation x27, other arithmetic, upper_of(): return jnp.linalg.cholesky(gram).T  138 us
    another operation x7, other arithmetic, on_device(): lead_factor = jnp.linalg.cholesky(lead_gram)  34.7 us
    psum x1, waiting for transfers between devices, on_device(): projected = lax.psum(partial_proj, 'row')  34.7 us
    another operation x2, other arithmetic, on_device(): jax.scipy.linalg.cho_solve((lead_factor, True), jnp.dot(lead.T, projected...  22.2 us
    another operation x3, other arithmetic, apply_inverse(): return jax.scipy.linalg.solve_triangular(upper.T, rows.T, lower=True).T  19.7 us
  transfers between devices with their start and end apart: 6, of which 6 were waited for; matrix products, arithmetic and copies ran while one was open for 6% of the time, Pallas kernels for 0%

commit v1 on v0

--- a/solution.py
+++ b/solution.py
@@ -57,7 +57,11 @@
     vectors, lead = factor(panel)
     vectors, lead = (broadcast(vectors, "col", 0), broadcast(lead, "col", 0))
     partial_proj = lax.dot_general(vectors, matrix, (((0,), (0,)), ((), ())), precision=HIGHEST)
-    projected = lax.psum(partial_proj, "row")
+    projected = partial_proj
+    for hop in (1, 2, 4):
+        projected = projected + lax.ppermute(
+            projected, "row", [(dev, dev ^ hop) for dev in range(8)]
+        )
     lead_gram = jnp.dot(lead.T, lead, precision=HIGHEST)
     lead_factor = jnp.linalg.cholesky(lead_gram)
     coeffs = jax.scipy.linalg.cho_solve(

time: 593 us -> 571 us (0.963)
  waiting for transfers between devices: 270 us -> 242 us
    psum x1 -> x0, waiting for transfers between devices: 34.7 us -> none  [on_device(): projected = lax.psum(partial_proj, 'row')]
    ppermute x0 -> x3, waiting for transfers between devices: none -> 7.08 us  [on_device(): lax.ppermute(projected, 'row', [(dev, dev ^ hop) for dev in range(8)])]
  transfers between devices with their start and end apart: 6 -> 8, of which waited for: 6 -> 6; matrix products, arithmetic and copies ran while one was open for 6% -> 8% of each run, Pallas kernels for 0% -> 0%
where the time goes in v1:
time: 571 us; the launch traced here: 560 us
  waiting for transfers between devices  242 us (42%)
  other arithmetic  221 us (39%)
  matrix products  47.8 us (8%)
  between operations  20.8 us (4%)
  local copies, waits for them, and re-layouts  16.7 us (3%)
  starting transfers between devices  10.1 us (2%)
    psum x2, waiting for transfers between devices, broadcast(): return lax.psum(kept, axis)  226 us
    another operation x27, other arithmetic, upper_of(): return jnp.linalg.cholesky(gram).T  138 us
    another operation x7, other arithmetic, on_device(): lead_factor = jnp.linalg.cholesky(lead_gram)  34.6 us
    another operation x2, other arithmetic, on_device(): jax.scipy.linalg.cho_solve((lead_factor, True), jnp.dot(lead.T, projected...  21.2 us
    another operation x3, other arithmetic, apply_inverse(): return jax.scipy.linalg.solve_triangular(upper.T, rows.T, lower=True).T  19.7 us
  transfers between devices with their start and end apart: 8, of which 6 were waited for; matrix products, arithmetic and copies ran while one was open for 8% of the time, Pallas kernels for 0%

profile of v1, /device:TPU:8, one launch (start us, length us, event | category | flops | bytes accessed | tf_op | source)
XLA Modules:
  0.0 559.6 jit_solution(2932024004785954082)
XLA Ops:
  6.5 7.9 %fusion.1 = f32[256,256]{1,0:T(8,128)S(1)} fusion(f32[3072,384]{1,0:T(8,128)} %param.4), kind=kOutput, calls=%fused_computation.11 | convolution fusion | flops 2415919104 | bytes 3407872 | tf_op jit(solution)/shard_map/dot_general | solution.py:41
  14.7 11.7 %cholesky.256 = f32[128,128]{1,0:T(8,128)S(1)} custom-call(f32[128,128]{1,0:T(8,128)S(1)} %cholesky.422), custom_call_target="Cholesky" | custom-call | tf_op jit(solution)/shard_map/jit(cholesky)/cholesky | solution.py:26
  26.4 9.8 %custom-call.25 = f32[1,128,128]{1,2,0:T(8,128)S(1)} custom-call(f32[1,128,128]{2,1,0:T(8,128)S(1)} %get-tuple-element.77), custom_call_target="InvertDiagBlocksLowerTriangular" | custom-call | tf_op jit(solution)/shard_map/jit(cholesky)/cholesky | solution.py:26
  36.8 12.1 %cholesky.273 = f32[128,128]{1,0:T(8,128)S(1)} custom-call(f32[128,128]{1,0:T(8,128)S(1)} %convolution_subtract_fusion.4), custom_call_target="Cholesky" | custom-call | tf_op jit(solution)/shard_map/jit(cholesky)/cholesky | solution.py:26
  51.5 1.1 collective-permute-done
  53.2 11.7 %cholesky.290 = f32[128,128]{1,0:T(8,128)S(1)} custom-call(f32[128,128]{1,0:T(8,128)S(1)} %cholesky.425), custom_call_target="Cholesky" | custom-call | tf_op jit(solution)/shard_map/jit(cholesky)/cholesky | solution.py:26
  65.0 9.8 %custom-call.26 = f32[1,128,128]{1,2,0:T(8,128)S(1)} custom-call(f32[1,128,128]{2,1,0:T(8,128)S(1)} %get-tuple-element.73), custom_call_target="InvertDiagBlocksLowerTriangular" | custom-call | tf_op jit(solution)/shard_map/jit(cholesky)/cholesky | solution.py:26
  75.3 11.7 %cholesky.307 = f32[128,128]{1,0:T(8,128)S(1)} custom-call(f32[128,128]{1,0:T(8,128)S(1)} %slice_subtract_fusion.4), custom_call_target="Cholesky" | custom-call | tf_op jit(solution)/shard_map/jit(cholesky)/cholesky | solution.py:26
  89.7 1.7 collective-permute-start.1
  91.5 3.8 slice_bitcast_fusion
  95.7 2.7 collective-permute-done.1
  99.0 11.7 %cholesky.324 = f32[128,128]{1,0:T(8,128)S(1)} custom-call(f32[128,128]{1,0:T(8,128)S(1)} %cholesky.428), custom_call_target="Cholesky" | custom-call | tf_op jit(solution)/shard_map/jit(cholesky)/cholesky | solution.py:26
  110.7 9.8 %custom-call.27 = f32[1,128,128]{1,2,0:T(8,128)S(1)} custom-call(f32[1,128,128]{2,1,0:T(8,128)S(1)} %get-tuple-element.69), custom_call_target="InvertDiagBlocksLowerTriangular" | custom-call | tf_op jit(solution)/shard_map/jit(cholesky)/cholesky | solution.py:26
  121.0 11.7 %cholesky.341 = f32[128,128]{1,0:T(8,128)S(1)} custom-call(f32[128,128]{1,0:T(8,128)S(1)} %slice_subtract_fusion.3), custom_call_target="Cholesky" | custom-call | tf_op jit(solution)/shard_map/jit(cholesky)/cholesky | solution.py:26
  135.4 3.3 collective-permute-start.2
  139.2 5.5 collective-permute-done.2
  145.3 11.7 %cholesky.358 = f32[128,128]{1,0:T(8,128)S(1)} custom-call(f32[128,128]{1,0:T(8,128)S(1)} %cholesky.431), custom_call_target="Cholesky" | custom-call | tf_op jit(solution)/shard_map/jit(cholesky)/cholesky | solution.py:26
  157.1 9.8 %custom-call.28 = f32[1,128,128]{1,2,0:T(8,128)S(1)} custom-call(f32[1,128,128]{2,1,0:T(8,128)S(1)} %get-tuple-element.65), custom_call_target="InvertDiagBlocksLowerTriangular" | custom-call | tf_op jit(solution)/shard_map/jit(cholesky)/cholesky | solution.py:26
  167.4 11.7 %cholesky.375 = f32[128,128]{1,0:T(8,128)S(1)} custom-call(f32[128,128]{1,0:T(8,128)S(1)} %slice_subtract_fusion.2), custom_call_target="Cholesky" | custom-call | tf_op jit(solution)/shard_map/jit(cholesky)/cholesky | solution.py:26
  181.8 4.2 while.3
  182.8 1.3 bitcast_dynamic-update-slice_fusion.4
  184.7 1.3 bitcast_dynamic-update-slice_fusion.4
  186.0 19.7 %custom-call.19 = f32[2,128,128]{1,2,0:T(8,128)S(1)} custom-call(f32[2,128,128]{2,1,0:T(8,128)S(1)} %get-tuple-element.25), custom_call_target="InvertDiagBlocksLowerTriangular" | custom-call | tf_op jit(solution)/shard_map/jit(_solve_triangular)/triangular_solve | solution.py:37
  205.7 2.9 fusion.3
  208.6 5.2 convolution_subtract_fusion.1
  214.2 2.8 fusion.41
  218.0 1.7 copy-done
  219.9 1.9 broadcast_select_fusion
  221.8 66.3 %all-reduce.5.cloned.1.call-done = f32[256,256]{1,0:T(8,128)} async-done(((f32[256,256]{1,0:T(8,128)}), f32[256,256]{1,0:T(8,128)}) %all-reduce.5.cloned.1.call-update) | async-done | bytes 262160 | tf_op jit(solution)/shard_map/psum | solution.py:22
  288.1 1.7 fusion.12
  289.8 159.6 %all-reduce.7.cloned.1.call-done = (f32[3072,256]{1,0:T(8,128)}, f32[256,256]{1,0:T(8,128)}) async-done(((f32[3072,256]{1,0:T(8,128)}, f32[256,256]{1,0:T(8,128)}), (f32[3072,256]{1,0:T(8,128)}, f32[256,256]{1,0:T(8,128)})) %all-reduce.7.cloned.1.call-update) | async-done | bytes 3407888 | tf_op jit(solution)/shard_map/psum | solution.py:22
  449.4 1.6 fusion.81
  451.2 11.7 %cholesky.392 = f32[128,128]{1,0:T(8,128)S(1)} custom-call(f32[128,128]{1,0:T(8,128)S(1)} %cholesky.434), custom_call_target="Cholesky" | custom-call | tf_op jit(solution)/shard_map/jit(cholesky)/cholesky | solution.py:66
  463.0 9.8 %custom-call.29 = f32[1,128,128]{1,2,0:T(8,128)S(1)} custom-call(f32[1,128,128]{2,1,0:T(8,128)S(1)} %get-tuple-element.61), custom_call_target="InvertDiagBlocksLowerTriangular" | custom-call | tf_op jit(solution)/shard_map/jit(cholesky)/cholesky | solution.py:66
  472.8 8.7 %fusion.82 = f32[256,384]{1,0:T(8,128)S(1)} fusion(f32[3072,256]{1,0:T(8,128)} %get-tuple-element.50, f32[3072,384]{1,0:T(8,128)} %param.4), kind=kOutput, calls=%fused_computation.154 | convolution fusion | flops 3623878656 | bytes 8257536 | tf_op jit(solution)/shard_map/dot_general | solution.py:59
  482.1 11.7 %cholesky.409 = f32[128,128]{1,0:T(8,128)S(1)} custom-call(f32[128,128]{1,0:T(8,128)S(1)} %convolution_subtract_fusion.3), custom_call_target="Cholesky" | custom-call | tf_op jit(solution)/shard_map/jit(cholesky)/cholesky | solution.py:66
  494.7 1.5 collective-permute-start.4
  499.4 7.1 %collective-permute-done.4 = f32[256,384]{1,0:T(8,128)} collective-permute-done((f32[256,384]{1,0:T(8,128)}, f32[256,384]{1,0:T(8,128)}, u32[]{:S(2)}, u32[]{:S(2)}) %collective-permute-start.4) | collective-permute-done | bytes 393248 | tf_op jit(solution)/shard_map/ppermute | solution.py:62
  506.5 1.9 add.65
  508.4 3.2 collective-permute-start.5
  511.6 5.6 while.4
  512.3 2.2 bitcast_dynamic-update-slice_fusion.5
  515.1 2.1 bitcast_dynamic-update-slice_fusion.5
  517.9 20.5 %custom-call.20 = f32[2,128,128]{1,2,0:T(8,128)S(1)} custom-call(f32[2,128,128]{2,1,0:T(8,128)} %copy-done.3), custom_call_target="InvertDiagBlocksLowerTriangular" | custom-call | tf_op jit(solution)/shard_map/jit(_cho_solve)/triangular_solve | solution.py:67
  538.4 1.7 fusion.8
  540.5 1.2 fusion.70
  542.4 1.2 convolution_subtract_fusion.2
  543.9 8.4 %convolution_subtract_fusion = f32[3072,384]{1,0:T(8,128)} fusion(f32[3072,384]{1,0:T(8,128)} %param.4, f32[3072,256]{1,0:T(8,128)S(1)} %copy-done.1, f32[128,384]{1,0:T(8,128)S(1)} %fusion.68, f32[128,384]{1,0:T(8,128)S(1)} %fusion.67), kind=kOutput, calls=%fused_computation.4 | convolution fusion | flops 3625156608 | bytes 12976128 | tf_op jit(solution)/shard_map/dot_general | solution.py:70
  (95 shorter events, 20.2 us)
Async XLA Ops:
  6.5 281.6 %all-reduce.5.cloned.1.call-start = ((), (), s32[]{:S(2)}) async-start(), calls=%async_computation | async-start | bytes 524288 | tf_op jit(solution)/shard_map/psum | solution.py:22
  51.0 1.6 collective-permute-start
  89.7 8.6 %collective-permute-start.1 = (f32[256,256]{0,1:T(8,128)S(1)}, f32[256,256]{0,1:T(8,128)S(1)}, u32[]{:S(2)}, u32[]{:S(2)}) collective-permute-start(f32[256,256]{0,1:T(8,128)S(1)} %fusion.22), channel_id=1, source_target_pairs={{0,64},{64,0},{32,96},{96,32},{128,192},{192,128},{160,224},{224,1... | collective-permute-start | bytes 786440 | tf_op jit(solution)/shard_map/ppermute | solution.py:17
  135.4 9.3 %collective-permute-start.2 = (f32[256,256]{0,1:T(8,128)S(1)}, f32[256,256]{0,1:T(8,128)S(1)}, u32[]{:S(2)}, u32[]{:S(2)}) collective-permute-start(f32[256,256]{0,1:T(8,128)S(1)} %fusion.24), channel_id=1, source_target_pairs={{0,128},{128,0},{32,160},{160,32},{64,192},{192,64},{96,224},{224,... | collective-permute-start | bytes 786440 | tf_op jit(solution)/shard_map/ppermute | solution.py:17
  218.0 1.7 copy-start
  219.7 229.7 %all-reduce.7.cloned.1.call-start = ((), (), s32[]{:S(2)}) async-start(), calls=%async_computation.1 | async-start | bytes 6815744 | tf_op jit(solution)/shard_map/psum | solution.py:22
  481.5 56.8 %copy-start.2 = (f32[256,256]{1,0:T(8,128)S(1)}, f32[256,256]{1,0:T(8,128)}, u32[]{:S(2)}) copy-start(f32[256,256]{1,0:T(8,128)} %get-tuple-element.51) | copy-start | bytes 786436
  481.5 12.3 %collective-permute-start.3 = (f32[256,384]{1,0:T(8,128)S(1)}, f32[256,384]{1,0:T(8,128)S(1)}, u32[]{:S(2)}, u32[]{:S(2)}) collective-permute-start(f32[256,384]{1,0:T(8,128)S(1)} %fusion.82), channel_id=1, source_target_pairs={{0,32},{32,0},{64,96},{96,64},{128,160},{160,128},{192,224},{224,1... | collective-permute-start | bytes 1179656 | tf_op jit(solution)/shard_map/ppermute | solution.py:62
  494.7 11.8 %collective-permute-start.4 = (f32[256,384]{1,0:T(8,128)}, f32[256,384]{1,0:T(8,128)}, u32[]{:S(2)}, u32[]{:S(2)}) collective-permute-start(f32[256,384]{1,0:T(8,128)} %add.64), channel_id=1, source_target_pairs={{0,64},{32,96},{64,0},{96,32},{128,192},{160,224},{192,128},{224,1... | collective-permute-start | bytes 1179656 | tf_op jit(solution)/shard_map/ppermute | solution.py:62
  499.4 44.5 %copy-start.1 = (f32[3072,256]{1,0:T(8,128)S(1)}, f32[3072,256]{1,0:T(8,128)}, u32[]{:S(2)}) copy-start(f32[3072,256]{1,0:T(8,128)} %get-tuple-element.50) | copy-start | bytes 9437188
  508.4 30.0 %collective-permute-start.5 = (f32[256,384]{1,0:T(8,128)}, f32[256,384]{1,0:T(8,128)}, u32[]{:S(2)}, u32[]{:S(2)}) collective-permute-start(f32[256,384]{1,0:T(8,128)} %add.65), channel_id=1, source_target_pairs={{0,128},{32,160},{64,192},{96,224},{128,0},{160,32},{192,64},{224,... | collective-permute-start | bytes 1179656 | tf_op jit(solution)/shard_map/ppermute | solution.py:62
  517.2 0.7 copy-start.3
Sparse Core Ops, SparseCore 0:
  219.8 68.2 all-reduce.4
  291.8 157.5 all-reduce.6
